TPU v7x, 512 devices: a whole 4x8x8 slice. The times are simulated.
512 devices in a mesh: gx: 32 (over x, z), gy: 8 (over y_lo, core), phys: 2 (over y_hi).
Axes of the slice: x: 4, y: 8 (y_hi: 2, y_lo: 4; y = y_hi * 4 + y_lo), z: 8, core: 2. Of those that a mesh axis runs over, the one named last changes fastest.
Arguments:
- mech_load: float32 [32, 8, 2, 128, 768], P('gx', 'gy', 'phys'), may hold values from -63 to 63
- heat_load: float32 [32, 8, 2, 128, 256], P('gx', 'gy', 'phys'), may hold values from -63 to 63
- mech_factor: bfloat16 [32, 8, 2, 768, 768], P('gx', 'gy', 'phys'), may hold values from -0.21875 to 0.21875
- heat_factor: bfloat16 [32, 8, 2, 256, 256], P('gx', 'gy', 'phys'), may hold values from -0.375 to 0.375
- mech_diag: float32 [32, 8, 2, 768], P('gx', 'gy', 'phys'), may hold values from 0.1 to 1
- heat_diag: float32 [32, 8, 2, 256], P('gx', 'gy', 'phys'), may hold values from 0.1 to 1
- mech_wx: float32 [32, 8, 2, 768], P('gx', 'gy', 'phys'), may hold values from 0.5 to 4
- mech_wy: float32 [32, 8, 2, 768], P('gx', 'gy', 'phys'), may hold values from 0.5 to 4
- mech_wp: float32 [32, 8, 768], P('gx', 'gy'), may hold values from 0.5 to 4
- heat_wx: float32 [32, 8, 2, 256], P('gx', 'gy', 'phys'), may hold values from 0.5 to 4
- heat_wy: float32 [32, 8, 2, 256], P('gx', 'gy', 'phys'), may hold values from 0.5 to 4
- heat_wp: float32 [32, 8, 256], P('gx', 'gy'), may hold values from 0.5 to 4
- coupling: bfloat16 [32, 8, 2, 768, 256], P('gx', 'gy', 'phys'), may hold values from -0.21875 to 0.21875
- mech_sens: bfloat16 [32, 8, 2, 768, 256], P('gx', 'gy', 'phys'), may hold values from -0.21875 to 0.21875
- heat_sens: bfloat16 [32, 8, 2, 256, 256], P('gx', 'gy', 'phys'), may hold values from -0.375 to 0.375
- density: float32 [32, 8, 256], P('gx', 'gy', 'phys'), may hold values from 0.2 to 1
- material_ids: int32 [32, 8, 256], P('gx', 'gy', 'phys'), may hold values from 0 to 7
- material_scale: float32 [8], replicated, may hold values from 1 to 10
Outputs:
- mech_adjoint: float32 [32, 8, 2, 128, 768], P('gx', 'gy', 'phys')
- heat_adjoint: float32 [32, 8, 2, 128, 256], P('gx', 'gy', 'phys')
- gradient: float32 [32, 8, 256], P('gx', 'gy', 'phys')
All inputs are finite; a program needn't handle non-finite values.
Results may differ from a plain program's by a relative error of at most 0.014.
Values may be sent and summed in bfloat16 or wider, within the bound.
A program may use at most 64 MiB of HBM per device.

v0:
```python
import jax
import jax.numpy as jnp
from jax import lax
from jax.sharding import PartitionSpec as P

LOADS = 128
ITERS = 2


def with_halo(array, sides, width):
    for axis, dim in sides:
        devices, length = (lax.axis_size(axis), array.shape[dim])
        up = [(i, (i + 1) % devices) for i in range(devices - 1)]
        down = [(j, i) for i, j in up]
        last = lax.slice_in_dim(array, length - width, length, axis=dim)
        initial = lax.slice_in_dim(array, 0, width, axis=dim)
        before = lax.ppermute(last, axis, up)
        after = lax.ppermute(initial, axis, down)
        array = jnp.concatenate([before, array, after], axis=dim)
    return array


def from_partner(array, axis, apart):
    return lax.ppermute(array, axis, [(i, i ^ 1 << apart) for i in range(lax.axis_size(axis))])


def from_behind(array, axis, by):
    devices = lax.axis_size(axis)
    pairs = [(i, i + by) for i in range(devices) if 0 <= i + by < devices]
    return lax.ppermute(array, axis, pairs)


def apply_operator(rounded, coefs, thermal):
    factor, diagonal, lower_x, upper_x, lower_y, upper_y, partner_weight = coefs
    block = rounded[None, None, None]
    if thermal:
        padded = with_halo(block, (("gx", 0), ("gy", 1)), 1)
        partner = from_partner(rounded, "phys", 0)
    else:
        padded = with_halo(block, (("gx", 0), ("gy", 1)), 1)
        partner = from_partner(rounded, "phys", 0)
    middle = 0
    western = padded[0, 1, middle].astype(jnp.float32)
    eastern = padded[2, 1, middle].astype(jnp.float32)
    southern = padded[1, 0, middle].astype(jnp.float32)
    northern = padded[1, 2, middle].astype(jnp.float32)
    inner = jnp.dot(rounded, factor, preferred_element_type=jnp.float32).astype(jnp.bfloat16)
    schur = lax.dot_general(
        inner, factor, (((1,), (1,)), ((), ())), preferred_element_type=jnp.float32
    )
    values = rounded.astype(jnp.float32)
    image = schur + diagonal * values
    image = image + lower_x * (values - western) + upper_x * (values - eastern)
    image = image + lower_y * (values - southern) + upper_y * (values - northern)
    image = image + partner_weight * (values - partner.astype(jnp.float32))
    return image


def interface_solve(load, coefs, thermal):
    solution = jnp.zeros_like(load)
    residual = load
    direction = load
    if thermal:
        current = lax.psum(jnp.sum(load * load, axis=1), ("gx", "gy", "phys"))
    else:
        current = lax.psum(jnp.sum(load * load, axis=1), ("gx", "gy", "phys"))
    for iteration in range(ITERS):
        rounded = direction.astype(jnp.bfloat16)
        image = apply_operator(rounded, coefs, thermal)
        local_curv = jnp.sum(rounded.astype(jnp.float32) * image, axis=1)
        if thermal:
            curvature = lax.psum(local_curv, ("gx", "gy", "phys"))
        else:
            curvature = lax.psum(local_curv, ("gx", "gy", "phys"))
        alpha = current / curvature
        solution = solution + alpha[:, None] * direction
        if iteration + 1 < ITERS:
            residual = residual - alpha[:, None] * image
            if thermal:
                following = lax.psum(jnp.sum(residual * residual, axis=1), ("gx", "gy", "phys"))
            else:
                following = lax.psum(jnp.sum(residual * residual, axis=1), ("gx", "gy", "phys"))
            direction = residual + (following / current)[:, None] * direction
            current = following
    return solution


def on_device(
    mech_load,
    heat_load,
    mech_factor,
    heat_factor,
    mech_diag,
    heat_diag,
    mech_wx,
    mech_wy,
    mech_wp,
    heat_wx,
    heat_wy,
    heat_wp,
    coupling,
    mech_sens,
    heat_sens,
    density,
    material_ids,
    material_scale,
):
    mech_width = mech_load.shape[-1]
    lower_rows = jnp.concatenate([mech_wx[0, 0, 0], heat_wx[0, 0, 0]])
    lower_cols = jnp.concatenate([mech_wy[0, 0, 0], heat_wy[0, 0, 0]])
    upper_rows = from_behind(lower_rows, "gx", -1)
    upper_cols = from_behind(lower_cols, "gy", -1)
    mech_coefs = (
        mech_factor[0, 0, 0],
        mech_diag[0, 0, 0],
        mech_wx[0, 0, 0],
        upper_rows[:mech_width],
        mech_wy[0, 0, 0],
        upper_cols[:mech_width],
        mech_wp[0, 0],
    )
    mech_adjoint = interface_solve(mech_load[0, 0, 0], mech_coefs, False)
    coupled = jnp.dot(
        mech_adjoint.astype(jnp.bfloat16), coupling[0, 0, 0], preferred_element_type=jnp.float32
    )
    heat_source = heat_load[0, 0, 0] - coupled
    heat_coefs = (
        heat_factor[0, 0, 0],
        heat_diag[0, 0, 0],
        heat_wx[0, 0, 0],
        upper_rows[mech_width:],
        heat_wy[0, 0, 0],
        upper_cols[mech_width:],
        heat_wp[0, 0],
    )
    heat_adjoint = interface_solve(heat_source, heat_coefs, True)
    mech_energy = jnp.sum(mech_adjoint * mech_adjoint, axis=0).astype(jnp.bfloat16)
    heat_energy = jnp.sum(heat_adjoint * heat_adjoint, axis=0).astype(jnp.bfloat16)
    partial_sens = jnp.dot(mech_energy, mech_sens[0, 0, 0], preferred_element_type=jnp.float32)
    partial_sens = partial_sens + jnp.dot(
        heat_energy, heat_sens[0, 0, 0], preferred_element_type=jnp.float32
    )
    summed = lax.psum(partial_sens, "phys")
    stride = partial_sens.shape[0] // lax.axis_size("phys")
    portion = lax.dynamic_slice_in_dim(summed, lax.axis_index("phys") * stride, stride, 0)
    onehot = (
        material_ids[0, 0][:, None] == jnp.arange(material_scale.shape[0], dtype=jnp.int32)[None, :]
    ).astype(jnp.float32)
    stiffness = jnp.dot(onehot, material_scale, precision=lax.Precision.HIGHEST)
    densities = density[0, 0]
    gradient = -3.0 * densities * densities * stiffness * portion / LOADS
    return (mech_adjoint[None, None, None], heat_adjoint[None, None, None], gradient[None, None])


def solution(mesh):
    placed = (
        P("gx", "gy", "phys", None, None),
        P("gx", "gy", "phys", None, None),
        P("gx", "gy", "phys", None, None),
        P("gx", "gy", "phys", None, None),
        P("gx", "gy", "phys", None),
        P("gx", "gy", "phys", None),
        P("gx", "gy", "phys", None),
        P("gx", "gy", "phys", None),
        P("gx", "gy", None),
        P("gx", "gy", "phys", None),
        P("gx", "gy", "phys", None),
        P("gx", "gy", None),
        P("gx", "gy", "phys", None, None),
        P("gx", "gy", "phys", None, None),
        P("gx", "gy", "phys", None, None),
        P("gx", "gy", "phys"),
        P("gx", "gy", "phys"),
        P(),
    )
    return jax.shard_map(
        on_device,
        mesh=mesh,
        in_specs=placed,
        out_specs=(
            P("gx", "gy", "phys", None, None),
            P("gx", "gy", "phys", None, None),
            P("gx", "gy", "phys"),
        ),
        check_vma=False,
    )
```

profile of v0, /device:TPU:1, one launch (start us, length us, event | category | flops | bytes accessed | tf_op | source)
XLA Modules:
  0.0 722.6 jit_solution(3888469934136934606)
XLA Ops:
  2.0 4.8 collective-permute-start
  9.4 4.5 collective-permute-done.2
  13.9 5.9 collective-permute-start.3
  19.8 2.0 collective-permute-start.5
  23.8 6.5 collective-permute-start.6
  31.9 3.9 collective-permute-done.1
  36.2 2.0 fusion.30
  38.1 107.8 %all-reduce.1 = (f32[128]{0:T(128)S(1)}, f32[128]{0:T(128)S(1)}) all-reduce(f32[128]{0:T(128)S(1)} %fusion.44, f32[128]{0:T(128)S(1)} %get-tuple-element.15), channel_id=1, replica_groups=mesh['gx'=32,'gy'=8,'phys'=2] {'gx','gy','phys'}, use_global_device_ids=true, to_apply=%region_1.0 | all-reduce | flops 256 | bytes 2048 | tf_op jit(solution)/shard_map/psum | solution.py:66
  146.1 94.5 %psum.65 = f32[128]{0:T(128)S(1)} all-reduce(f32[128]{0:T(128)S(1)} %multiply_reduce_fusion.1), channel_id=1, replica_groups=mesh['gx'=32,'gy'=8,'phys'=2] {'gx','gy','phys'}, use_global_device_ids=true, to_apply=%region_5.0 | all-reduce | flops 128 | bytes 1024 | tf_op jit(solution)/shard_map/psum | solution.py:82
  240.8 2.7 collective-permute-start.7
  244.8 2.2 collective-permute-done.7
  247.1 3.8 collective-permute-done.8
  250.9 3.8 collective-permute-start.10
  254.7 1.9 collective-permute-start.9
  256.7 4.7 collective-permute-start.11
  262.1 11.8 %collective-permute-done.11 = bf16[128,768]{1,0:T(8,128)(2,1)} collective-permute-done((bf16[128,768]{1,0:T(8,128)(2,1)S(1)}, bf16[128,768]{1,0:T(8,128)(2,1)}, u32[]{:S(2)}, u32[]{:S(2)}) %collective-permute-start.11) | collective-permute-done | bytes 196640 | tf_op jit(solution)/shard_map/ppermute | solution.py:24
  275.6 98.5 %psum.66 = f32[128]{0:T(128)S(1)} all-reduce(f32[128]{0:T(128)S(1)} %fusion.47), channel_id=1, replica_groups=mesh['gx'=32,'gy'=8,'phys'=2] {'gx','gy','phys'}, use_global_device_ids=true, to_apply=%region_7.0 | all-reduce | flops 128 | bytes 1024 | tf_op jit(solution)/shard_map/psum | solution.py:74
  374.7 3.4 collective-permute-start.12
  379.4 3.7 collective-permute-done.13
  383.1 2.9 collective-permute-start.14
  386.1 2.4 collective-permute-start.15
  388.5 4.4 collective-permute-start.16
  394.3 3.8 collective-permute-done.16
  399.6 99.2 %all-reduce = (f32[128]{0:T(128)S(1)}, f32[128]{0:T(128)S(1)}) all-reduce(f32[128]{0:T(128)S(1)} %get-tuple-element.13, f32[128]{0:T(128)S(1)} %get-tuple-element.18), channel_id=1, replica_groups=mesh['gx'=32,'gy'=8,'phys'=2] {'gx','gy','phys'}, use_global_device_ids=true, to_apply=%region_9.0 | all-reduce | flops 256 | bytes 2048 | tf_op jit(solution)/shard_map/psum | solution.py:64
  499.0 95.5 %psum.69 = f32[128]{0:T(128)S(1)} all-reduce(f32[128]{0:T(128)S(1)} %multiply_reduce_fusion.3), channel_id=1, replica_groups=mesh['gx'=32,'gy'=8,'phys'=2] {'gx','gy','phys'}, use_global_device_ids=true, to_apply=%region_13.0 | all-reduce | flops 128 | bytes 1024 | tf_op jit(solution)/shard_map/psum | solution.py:80
  594.6 3.3 collective-permute-start.17
  599.3 4.6 collective-permute-start.21
  603.9 2.1 collective-permute-start.19
  606.0 2.3 collective-permute-start.20
  609.4 3.6 collective-permute-done.20
  613.4 99.8 %psum.70 = f32[128]{0:T(128)S(1)} all-reduce(f32[128]{0:T(128)S(1)} %fusion.85), channel_id=1, replica_groups=mesh['gx'=32,'gy'=8,'phys'=2] {'gx','gy','phys'}, use_global_device_ids=true, to_apply=%region_15.0 | all-reduce | flops 128 | bytes 1024 | tf_op jit(solution)/shard_map/psum | solution.py:72
  714.1 7.7 %psum.71 = f32[256]{0:T(256)S(1)} all-reduce(f32[256]{0:T(256)S(1)} %add.136), channel_id=1, replica_groups=mesh['gx'=32,'gy'=8,'phys'=2] {'phys'}, use_global_device_ids=true, to_apply=%region_18.0 | all-reduce | flops 256 | bytes 2048 | tf_op jit(solution)/shard_map/psum | solution.py:143
  (115 shorter events, 21.3 us)
Async XLA Ops:
  2.0 7.4 %collective-permute-start = (bf16[1,1,1,128,768]{4,3,2,1,0:T(8,128)(2,1)S(1)}, bf16[1,1,1,128,768]{4,3,2,1,0:T(8,128)(2,1)S(1)}, u32[]{:S(2)}, u32[]{:S(2)}) collective-permute-start(bf16[1,1,1,128,768]{4,3,2,1,0:T(8,128)(2,1)S(1)} %get-tuple-element.11), channel_id=1, source_target_pairs={{0,16},{16,32},{32,48},{48,64},{64,80},{80,96},{96,112},{112,128},... | collective-permute-start | bytes 589832 | tf_op jit(solution)/shard_map/ppermute | solution.py:17
  6.8 7.0 collective-permute-start.2
  13.9 22.2 %collective-permute-start.3 = (bf16[3,1,1,128,768]{4,3,2,1,0:T(8,128)(2,1)S(1)}, bf16[3,1,1,128,768]{4,3,2,1,0:T(8,128)(2,1)}, u32[]{:S(2)}, u32[]{:S(2)}) collective-permute-start(bf16[3,1,1,128,768]{4,3,2,1,0:T(8,128)(2,1)S(1)} %pad_maximum_fusion), channel_id=1, source_target_pairs={{0,2},{2,4},{4,6},{6,8},{8,10},{10,12},{12,14},{1,3},{3,5},{5,7},{... | collective-permute-start | bytes 1769480 | tf_op jit(solution)/shard_map/ppermute | solution.py:17
  19.8 16.3 %collective-permute-start.5 = (bf16[3,1,1,128,768]{4,3,2,1,0:T(8,128)(2,1)S(1)}, bf16[3,1,1,128,768]{4,3,2,1,0:T(8,128)(2,1)}, u32[]{:S(2)}, u32[]{:S(2)}) collective-permute-start(bf16[3,1,1,128,768]{4,3,2,1,0:T(8,128)(2,1)S(1)} %pad_maximum_fusion), channel_id=1, source_target_pairs={{2,0},{4,2},{6,4},{8,6},{10,8},{12,10},{14,12},{3,1},{5,3},{7,5},{... | collective-permute-start | bytes 1769480 | tf_op jit(solution)/shard_map/ppermute | solution.py:18
  21.9 10.0 %collective-permute-start.4 = (f32[1024]{0:T(1024)S(1)}, f32[1024]{0:T(1024)S(1)}, u32[]{:S(2)}, u32[]{:S(2)}) collective-permute-start(f32[1024]{0:T(1024)S(1)} %pad_maximum_fusion.5), channel_id=1, source_target_pairs={{2,0},{4,2},{6,4},{8,6},{10,8},{12,10},{14,12},{3,1},{5,3},{7,5},{... | collective-permute-start | bytes 12296 | tf_op jit(solution)/shard_map/ppermute | solution.py:30
  23.8 12.3 %collective-permute-start.6 = (bf16[128,768]{1,0:T(8,128)(2,1)S(1)}, bf16[128,768]{1,0:T(8,128)(2,1)}, u32[]{:S(2)}, u32[]{:S(2)}) collective-permute-start(bf16[128,768]{1,0:T(8,128)(2,1)S(1)} %get-tuple-element.12), channel_id=1, source_target_pairs={{0,1},{1,0},{2,3},{3,2},{4,5},{5,4},{6,7},{7,6},{8,9},{9,8},{10,11... | collective-permute-start | bytes 589832 | tf_op jit(solution)/shard_map/ppermute | solution.py:24
  30.4 5.4 collective-permute-start.1
  31.9 215.2 %copy-start.7 = (f32[1024]{0:T(1024)}, f32[1024]{0:T(1024)S(1)}, u32[]{:S(2)}) copy-start(f32[1024]{0:T(1024)S(1)} %collective-permute-done.4) | copy-start | bytes 12292
  35.8 211.3 %copy-start.8 = (f32[1024]{0:T(1024)}, f32[1024]{0:T(1024)S(1)}, u32[]{:S(2)}) copy-start(f32[1024]{0:T(1024)S(1)} %collective-permute-done.1) | copy-start | bytes 12292
  145.9 101.1 %copy-start.9 = (f32[128]{0:T(128)}, f32[128]{0:T(128)S(1)}, u32[]{:S(2)}) copy-start(f32[128]{0:T(128)S(1)} %div.24) | copy-start | bytes 1540
  240.8 6.3 collective-permute-start.7
  243.5 7.3 %collective-permute-start.8 = (bf16[1,1,1,128,768]{4,3,2,1,0:T(8,128)(2,1)S(1)}, bf16[1,1,1,128,768]{4,3,2,1,0:T(8,128)(2,1)S(1)}, u32[]{:S(2)}, u32[]{:S(2)}) collective-permute-start(bf16[1,1,1,128,768]{4,3,2,1,0:T(8,128)(2,1)S(1)} %bitcast.187), channel_id=1, source_target_pairs={{16,0},{32,16},{48,32},{64,48},{80,64},{96,80},{112,96},{128,112},... | collective-permute-start | bytes 589832 | tf_op jit(solution)/shard_map/ppermute | solution.py:18
  250.9 23.0 %collective-permute-start.10 = (bf16[3,1,1,128,768]{4,3,2,1,0:T(8,128)(2,1)S(1)}, bf16[3,1,1,128,768]{4,3,2,1,0:T(8,128)(2,1)}, u32[]{:S(2)}, u32[]{:S(2)}) collective-permute-start(bf16[3,1,1,128,768]{4,3,2,1,0:T(8,128)(2,1)S(1)} %pad_maximum_fusion.1), channel_id=1, source_target_pairs={{2,0},{4,2},{6,4},{8,6},{10,8},{12,10},{14,12},{3,1},{5,3},{7,5},{... | collective-permute-start | bytes 1769480 | tf_op jit(solution)/shard_map/ppermute | solution.py:18
  254.7 19.2 %collective-permute-start.9 = (bf16[3,1,1,128,768]{4,3,2,1,0:T(8,128)(2,1)S(1)}, bf16[3,1,1,128,768]{4,3,2,1,0:T(8,128)(2,1)}, u32[]{:S(2)}, u32[]{:S(2)}) collective-permute-start(bf16[3,1,1,128,768]{4,3,2,1,0:T(8,128)(2,1)S(1)} %pad_maximum_fusion.1), channel_id=1, source_target_pairs={{0,2},{2,4},{4,6},{6,8},{8,10},{10,12},{12,14},{1,3},{3,5},{5,7},{... | collective-permute-start | bytes 1769480 | tf_op jit(solution)/shard_map/ppermute | solution.py:17
  256.7 17.3 %collective-permute-start.11 = (bf16[128,768]{1,0:T(8,128)(2,1)S(1)}, bf16[128,768]{1,0:T(8,128)(2,1)}, u32[]{:S(2)}, u32[]{:S(2)}) collective-permute-start(bf16[128,768]{1,0:T(8,128)(2,1)S(1)} %fusion.48), channel_id=1, source_target_pairs={{0,1},{1,0},{2,3},{3,2},{4,5},{5,4},{6,7},{7,6},{8,9},{9,8},{10,11... | collective-permute-start | bytes 589832 | tf_op jit(solution)/shard_map/ppermute | solution.py:24
  262.1 112.0 %copy-start.10 = (f32[128]{0:T(128)S(1)}, f32[128]{0:T(128)}, u32[]{:S(2)}) copy-start(f32[128]{0:T(128)} %copy-done.9) | copy-start | bytes 1540
  374.7 233.7 %copy-start.3 = (bf16[1,1,1,768,256]{4,3,2,1,0:T(8,128)(2,1)S(1)}, bf16[1,1,1,768,256]{4,3,2,1,0:T(8,128)(2,1)}, u32[]{:S(2)}) copy-start(bf16[1,1,1,768,256]{4,3,2,1,0:T(8,128)(2,1)} %param.31) | copy-start | bytes 1179652
  374.7 4.7 collective-permute-start.12
  378.1 5.0 collective-permute-start.13
  383.1 14.9 %collective-permute-start.14 = (bf16[3,1,1,128,256]{4,3,2,1,0:T(8,128)(2,1)S(1)}, bf16[3,1,1,128,256]{4,3,2,1,0:T(8,128)(2,1)S(1)}, u32[]{:S(2)}, u32[]{:S(2)}) collective-permute-start(bf16[3,1,1,128,256]{4,3,2,1,0:T(8,128)(2,1)S(1)} %pad_maximum_fusion.2), channel_id=1, source_target_pairs={{0,2},{2,4},{4,6},{6,8},{8,10},{10,12},{12,14},{1,3},{3,5},{5,7},{... | collective-permute-start | bytes 589832 | tf_op jit(solution)/shard_map/ppermute | solution.py:17
  386.1 12.0 %collective-permute-start.15 = (bf16[3,1,1,128,256]{4,3,2,1,0:T(8,128)(2,1)S(1)}, bf16[3,1,1,128,256]{4,3,2,1,0:T(8,128)(2,1)S(1)}, u32[]{:S(2)}, u32[]{:S(2)}) collective-permute-start(bf16[3,1,1,128,256]{4,3,2,1,0:T(8,128)(2,1)S(1)} %pad_maximum_fusion.2), channel_id=1, source_target_pairs={{2,0},{4,2},{6,4},{8,6},{10,8},{12,10},{14,12},{3,1},{5,3},{7,5},{... | collective-permute-start | bytes 589832 | tf_op jit(solution)/shard_map/ppermute | solution.py:18
  388.5 9.6 %collective-permute-start.16 = (bf16[128,256]{1,0:T(8,128)(2,1)S(1)}, bf16[128,256]{1,0:T(8,128)(2,1)S(1)}, u32[]{:S(2)}, u32[]{:S(2)}) collective-permute-start(bf16[128,256]{1,0:T(8,128)(2,1)S(1)} %get-tuple-element.14), channel_id=1, source_target_pairs={{0,1},{1,0},{2,3},{3,2},{4,5},{5,4},{6,7},{7,6},{8,9},{9,8},{10,11... | collective-permute-start | bytes 196616 | tf_op jit(solution)/shard_map/ppermute | solution.py:24
  398.1 214.9 %copy-start.21 = (bf16[1,1,1,256,256]{4,3,2,1,0:T(8,128)(2,1)S(1)}, bf16[1,1,1,256,256]{4,3,2,1,0:T(8,128)(2,1)}, u32[]{:S(2)}) copy-start(bf16[1,1,1,256,256]{4,3,2,1,0:T(8,128)(2,1)} %param.21) | copy-start | bytes 393220
  594.6 119.4 %copy-start.5 = (bf16[1,1,1,256,256]{4,3,2,1,0:T(8,128)(2,1)S(1)}, bf16[1,1,1,256,256]{4,3,2,1,0:T(8,128)(2,1)}, u32[]{:S(2)}) copy-start(bf16[1,1,1,256,256]{4,3,2,1,0:T(8,128)(2,1)} %param.32) | copy-start | bytes 393220
  594.6 9.3 %collective-permute-start.17 = (bf16[1,1,1,128,256]{4,3,2,1,0:T(8,128)(2,1)S(1)}, bf16[1,1,1,128,256]{4,3,2,1,0:T(8,128)(2,1)S(1)}, u32[]{:S(2)}, u32[]{:S(2)}) collective-permute-start(bf16[1,1,1,128,256]{4,3,2,1,0:T(8,128)(2,1)S(1)} %bitcast.190), channel_id=1, source_target_pairs={{0,16},{16,32},{32,48},{48,64},{64,80},{80,96},{96,112},{112,128},... | collective-permute-start | bytes 196616 | tf_op jit(solution)/shard_map/ppermute | solution.py:17
  597.9 6.0 collective-permute-start.18
  599.2 122.6 %copy-start.24 = (s32[1,1,128]{2,1,0:T(1,128)S(1)}, s32[1,1,128]{2,1,0:T(1,128)}, u32[]{:S(2)}) copy-start(s32[1,1,128]{2,1,0:T(1,128)} %param.34) | copy-start | bytes 1540
  599.2 122.6 %copy-start.25 = (f32[8]{0:T(128)S(1)}, f32[8]{0:T(128)}, u32[]{:S(2)}) copy-start(f32[8]{0:T(128)} %param.35) | copy-start | bytes 100
  599.2 122.5 %copy-start.26 = (f32[1,1,128]{2,1,0:T(1,128)S(1)}, f32[1,1,128]{2,1,0:T(1,128)}, u32[]{:S(2)}) copy-start(f32[1,1,128]{2,1,0:T(1,128)} %param.33) | copy-start | bytes 1540
  599.3 9.2 %collective-permute-start.21 = (bf16[128,256]{1,0:T(8,128)(2,1)S(1)}, bf16[128,256]{1,0:T(8,128)(2,1)S(1)}, u32[]{:S(2)}, u32[]{:S(2)}) collective-permute-start(bf16[128,256]{1,0:T(8,128)(2,1)S(1)} %fusion.86), channel_id=1, source_target_pairs={{0,1},{1,0},{2,3},{3,2},{4,5},{5,4},{6,7},{7,6},{8,9},{9,8},{10,11... | collective-permute-start | bytes 196616 | tf_op jit(solution)/shard_map/ppermute | solution.py:24
  603.9 5.5 collective-permute-start.19
  606.0 7.0 collective-permute-start.20
  (19 other events, 765.4 us)
where the time goes:
time: 724 us; the launch traced here: 723 us
  blocking collectives  603 us (83%)
  starting transfers between devices  66.2 us (9%)
  waiting for transfers between devices  39.9 us (6%)
    psum x2, blocking collectives, interface_solve(): current = lax.psum(jnp.sum(load * load, axis=1), ('gx', 'gy', 'phys'))  207 us
    psum x2, blocking collectives, interface_solve(): curvature = lax.psum(local_curv, ('gx', 'gy', 'phys'))  198 us
    psum x2, blocking collectives, interface_solve(): lax.psum(jnp.sum(residual * residual, axis=1), ('gx', 'gy', 'phys'))  190 us
    ppermute x8, starting transfers between devices, with_halo(): before = lax.ppermute(last, axis, up)  27.1 us
    ppermute x4, starting transfers between devices, from_partner(): lax.ppermute(array, axis, [(i, i ^ 1 << apart) for i in range(lax.axis_si...  20.2 us
    ppermute x4, waiting for transfers between devices, from_partner(): lax.ppermute(array, axis, [(i, i ^ 1 << apart) for i in range(lax.axis_si...  16 us
    ppermute x8, starting transfers between devices, with_halo(): after = lax.ppermute(initial, axis, down)  15.7 us
    ppermute x8, waiting for transfers between devices, with_halo(): after = lax.ppermute(initial, axis, down)  15.5 us
  transfers between devices with their start and end apart: 22, of which 11 were waited for; matrix products, arithmetic and copies ran while one was open for 0% of the time, Pallas kernels for 0%

commit v1 on v0

--- a/solution.py
+++ b/solution.py
@@ -69,7 +69,8 @@
         image = apply_operator(rounded, coefs, thermal)
         local_curv = jnp.sum(rounded.astype(jnp.float32) * image, axis=1)
         if thermal:
-            curvature = lax.psum(local_curv, ("gx", "gy", "phys"))
+            parts = lax.all_gather(local_curv, ("gx", "gy", "phys"), axis=0, tiled=False)
+            curvature = parts.sum(axis=0)
         else:
             curvature = lax.psum(local_curv, ("gx", "gy", "phys"))
         alpha = current / curvature

time: 724 us -> 3090 us (4.27)
  blocking collectives: 603 us -> 2970 us
    all_gather x0 -> x2, blocking collectives: none -> 2470 us  [interface_solve(): lax.all_gather(local_curv, ('gx', 'gy', 'phys'), axis=0, tiled=False)]
    psum x2 -> x1, blocking collectives: 198 us -> 98.5 us  [interface_solve(): curvature = lax.psum(local_curv, ('gx', 'gy', 'phys'))]
  transfers between devices with their start and end apart: 22 -> 22, of which waited for: 11 -> 10; matrix products, arithmetic and copies ran while one was open for 0% -> 0% of each run, Pallas kernels for 0% -> 0%
where the time goes in v1:
time: 3090 us; the launch traced here: 3080 us
  blocking collectives  2970 us (96%)
  starting transfers between devices  65 us (2%)
  waiting for transfers between devices  36.4 us (1%)
    all_gather x2, blocking collectives, interface_solve(): lax.all_gather(local_curv, ('gx', 'gy', 'phys'), axis=0, tiled=False)  2470 us
    psum x2, blocking collectives, interface_solve(): current = lax.psum(jnp.sum(load * load, axis=1), ('gx', 'gy', 'phys'))  208 us
    psum x2, blocking collectives, interface_solve(): lax.psum(jnp.sum(residual * residual, axis=1), ('gx', 'gy', 'phys'))  189 us
    psum x1, blocking collectives, interface_solve(): curvature = lax.psum(local_curv, ('gx', 'gy', 'phys'))  98.5 us
  transfers between devices with their start and end apart: 22, of which 10 were waited for; matrix products, arithmetic and copies ran while one was open for 0% of the time, Pallas kernels for 0%

profile of v1, /device:TPU:1, one launch (start us, length us, event | category | flops | bytes accessed | tf_op | source)
XLA Modules:
  0.0 3084.3 jit_solution(2373056938076089766)
XLA Ops:
  2.0 4.8 collective-permute-start
  9.4 4.5 collective-permute-done.2
  13.9 5.9 collective-permute-start.3
  19.8 2.0 collective-permute-start.5
  23.8 6.5 collective-permute-start.6
  31.9 3.9 collective-permute-done.1
  36.2 2.0 fusion.30
  38.1 107.8 %all-reduce = (f32[128]{0:T(128)S(1)}, f32[128]{0:T(128)S(1)}) all-reduce(f32[128]{0:T(128)S(1)} %fusion.44, f32[128]{0:T(128)S(1)} %get-tuple-element.13), channel_id=1, replica_groups=mesh['gx'=32,'gy'=8,'phys'=2] {'gx','gy','phys'}, use_global_device_ids=true, to_apply=%region_1.0 | all-reduce | flops 256 | bytes 2048 | tf_op jit(solution)/shard_map/psum | solution.py:66
  146.1 94.5 %psum.51 = f32[128]{0:T(128)S(1)} all-reduce(f32[128]{0:T(128)S(1)} %multiply_reduce_fusion.1), channel_id=1, replica_groups=mesh['gx'=32,'gy'=8,'phys'=2] {'gx','gy','phys'}, use_global_device_ids=true, to_apply=%region_5.0 | all-reduce | flops 128 | bytes 1024 | tf_op jit(solution)/shard_map/psum | solution.py:83
  240.8 2.7 collective-permute-start.7
  244.8 2.2 collective-permute-done.7
  247.1 3.8 collective-permute-done.8
  250.9 3.8 collective-permute-start.10
  254.7 1.9 collective-permute-start.9
  256.7 4.7 collective-permute-start.11
  262.1 11.8 collective-permute-done.11
  275.6 98.5 %psum.52 = f32[128]{0:T(128)S(1)} all-reduce(f32[128]{0:T(128)S(1)} %fusion.47), channel_id=1, replica_groups=mesh['gx'=32,'gy'=8,'phys'=2] {'gx','gy','phys'}, use_global_device_ids=true, to_apply=%region_7.0 | all-reduce | flops 128 | bytes 1024 | tf_op jit(solution)/shard_map/psum | solution.py:75
  374.7 3.2 collective-permute-start.12
  379.3 3.7 collective-permute-done.13
  383.0 2.9 collective-permute-start.14
  385.9 2.4 collective-permute-start.15
  388.3 4.4 collective-permute-start.16
  394.1 99.9 %psum.53 = f32[128]{0:T(128)S(1)} all-reduce(f32[128]{0:T(128)S(1)} %get-tuple-element.11), channel_id=1, replica_groups=mesh['gx'=32,'gy'=8,'phys'=2] {'gx','gy','phys'}, use_global_device_ids=true, to_apply=%region_9.0 | all-reduce | flops 128 | bytes 1024 | tf_op jit(solution)/shard_map/psum | solution.py:64
  494.6 1234.1 %all-gather.2 = f32[512,1,128]{2,1,0:T(1,128)S(1)} all-gather(f32[1,1,128]{2,1,0:T(1,128)S(1)} %bitcast.211), channel_id=2, replica_groups=mesh['gx'=32,'gy'=8,'phys'=2] {'gx','gy','phys'}, dimensions={0}, use_global_device_ids=true | all-gather | bytes 262656 | tf_op jit(solution)/shard_map/all_gather | solution.py:72
  1729.4 94.2 %psum.54 = f32[128]{0:T(128)S(1)} all-reduce(f32[128]{0:T(128)S(1)} %multiply_reduce_fusion.3), channel_id=1, replica_groups=mesh['gx'=32,'gy'=8,'phys'=2] {'gx','gy','phys'}, use_global_device_ids=true, to_apply=%region_13.0 | all-reduce | flops 128 | bytes 1024 | tf_op jit(solution)/shard_map/psum | solution.py:81
  1823.6 2.0 collective-permute-start.17
  1827.0 4.7 collective-permute-start.21
  1831.8 2.5 collective-permute-start.19
  1834.3 2.1 collective-permute-start.20
  1837.6 3.7 collective-permute-done.20
  1841.7 1232.7 %all-gather.3 = f32[512,1,128]{2,1,0:T(1,128)S(1)} all-gather(f32[1,1,128]{2,1,0:T(1,128)S(1)} %bitcast.212), channel_id=3, replica_groups=mesh['gx'=32,'gy'=8,'phys'=2] {'gx','gy','phys'}, dimensions={0}, use_global_device_ids=true | all-gather | bytes 262656 | tf_op jit(solution)/shard_map/all_gather | solution.py:72
  3075.9 7.7 psum.55
  (120 shorter events, 21.5 us)
Async XLA Ops:
  2.0 7.4 collective-permute-start
  6.8 7.0 collective-permute-start.2
  13.9 22.2 collective-permute-start.3
  19.8 16.3 collective-permute-start.5
  21.9 10.0 collective-permute-start.4
  23.8 12.3 collective-permute-start.6
  30.4 5.4 collective-permute-start.1
  31.9 215.2 %copy-start.7 = (f32[1024]{0:T(1024)}, f32[1024]{0:T(1024)S(1)}, u32[]{:S(2)}) copy-start(f32[1024]{0:T(1024)S(1)} %collective-permute-done.4) | copy-start | bytes 12292
  35.8 211.3 %copy-start.8 = (f32[1024]{0:T(1024)}, f32[1024]{0:T(1024)S(1)}, u32[]{:S(2)}) copy-start(f32[1024]{0:T(1024)S(1)} %collective-permute-done.1) | copy-start | bytes 12292
  240.8 6.3 collective-permute-start.7
  243.5 7.3 collective-permute-start.8
  250.9 23.0 collective-permute-start.10
  254.7 19.2 collective-permute-start.9
  256.7 17.3 collective-permute-start.11
  374.1 120.0 %copy-start.18 = (f32[1,1,1,256]{3,2,1,0:T(1,128)S(1)}, f32[1,1,1,256]{3,2,1,0:T(1,128)}, u32[]{:S(2)}) copy-start(f32[1,1,1,256]{3,2,1,0:T(1,128)} %param.28) | copy-start | bytes 3076
  374.3 120.2 %copy-start.2 = (f32[128,768]{1,0:T(8,128)}, f32[128,768]{1,0:T(8,128)S(1)}, u32[]{:S(2)}) copy-start(f32[128,768]{1,0:T(8,128)S(1)} %get-tuple-element.8) | copy-start | bytes 1179652
  374.7 4.6 collective-permute-start.12
  378.0 5.0 collective-permute-start.13
  383.0 111.1 %collective-permute-start.14 = (bf16[3,1,1,128,256]{4,3,2,1,0:T(8,128)(2,1)S(1)}, bf16[3,1,1,128,256]{4,3,2,1,0:T(8,128)(2,1)S(1)}, u32[]{:S(2)}, u32[]{:S(2)}) collective-permute-start(bf16[3,1,1,128,256]{4,3,2,1,0:T(8,128)(2,1)S(1)} %pad_maximum_fusion.2), channel_id=1, source_target_pairs={{0,2},{2,4},{4,6},{6,8},{8,10},{10,12},{12,14},{1,3},{3,5},{5,7},{... | collective-permute-start | bytes 589832 | tf_op jit(solution)/shard_map/ppermute | solution.py:17
  385.9 108.1 %collective-permute-start.15 = (bf16[3,1,1,128,256]{4,3,2,1,0:T(8,128)(2,1)S(1)}, bf16[3,1,1,128,256]{4,3,2,1,0:T(8,128)(2,1)S(1)}, u32[]{:S(2)}, u32[]{:S(2)}) collective-permute-start(bf16[3,1,1,128,256]{4,3,2,1,0:T(8,128)(2,1)S(1)} %pad_maximum_fusion.2), channel_id=1, source_target_pairs={{2,0},{4,2},{6,4},{8,6},{10,8},{12,10},{14,12},{3,1},{5,3},{7,5},{... | collective-permute-start | bytes 589832 | tf_op jit(solution)/shard_map/ppermute | solution.py:18
  388.3 105.7 %collective-permute-start.16 = (bf16[128,256]{1,0:T(8,128)(2,1)S(1)}, bf16[128,256]{1,0:T(8,128)(2,1)S(1)}, u32[]{:S(2)}, u32[]{:S(2)}) collective-permute-start(bf16[128,256]{1,0:T(8,128)(2,1)S(1)} %get-tuple-element.12), channel_id=1, source_target_pairs={{0,1},{1,0},{2,3},{3,2},{4,5},{5,4},{6,7},{7,6},{8,9},{9,8},{10,11... | collective-permute-start | bytes 196616 | tf_op jit(solution)/shard_map/ppermute | solution.py:24
  494.1 1342.3 %copy-start.3 = (bf16[1,1,1,768,256]{4,3,2,1,0:T(8,128)(2,1)S(1)}, bf16[1,1,1,768,256]{4,3,2,1,0:T(8,128)(2,1)}, u32[]{:S(2)}) copy-start(bf16[1,1,1,768,256]{4,3,2,1,0:T(8,128)(2,1)} %param.31) | copy-start | bytes 1179652
  494.5 1346.8 %copy-start.22 = (bf16[1,1,1,256,256]{4,3,2,1,0:T(8,128)(2,1)S(1)}, bf16[1,1,1,256,256]{4,3,2,1,0:T(8,128)(2,1)}, u32[]{:S(2)}) copy-start(bf16[1,1,1,256,256]{4,3,2,1,0:T(8,128)(2,1)} %param.21) | copy-start | bytes 393220
  1823.6 8.1 collective-permute-start.17
  1825.7 6.1 collective-permute-start.18
  1827.0 9.6 collective-permute-start.21
  1831.8 1244.0 %copy-start.5 = (bf16[1,1,1,256,256]{4,3,2,1,0:T(8,128)(2,1)S(1)}, bf16[1,1,1,256,256]{4,3,2,1,0:T(8,128)(2,1)}, u32[]{:S(2)}) copy-start(bf16[1,1,1,256,256]{4,3,2,1,0:T(8,128)(2,1)} %param.32) | copy-start | bytes 393220
  1831.8 1251.8 %copy-start.25 = (s32[1,1,128]{2,1,0:T(1,128)S(1)}, s32[1,1,128]{2,1,0:T(1,128)}, u32[]{:S(2)}) copy-start(s32[1,1,128]{2,1,0:T(1,128)} %param.34) | copy-start | bytes 1540
  1831.8 1251.8 %copy-start.26 = (f32[8]{0:T(128)S(1)}, f32[8]{0:T(128)}, u32[]{:S(2)}) copy-start(f32[8]{0:T(128)} %param.35) | copy-start | bytes 100
  1831.8 1251.8 %copy-start.27 = (f32[1,1,128]{2,1,0:T(1,128)S(1)}, f32[1,1,128]{2,1,0:T(1,128)}, u32[]{:S(2)}) copy-start(f32[1,1,128]{2,1,0:T(1,128)} %param.33) | copy-start | bytes 1540
  1831.8 5.8 collective-permute-start.19
  1834.3 7.0 collective-permute-start.20
  (20 other events, 1337.2 us)
